TPU v7x, 512 devices: a whole 4x4x16 slice. The times are simulated.
512 devices in a mesh: lon: 16 (over z), lat: 8 (over x_lo, y), ch: 4 (over x_hi, core).
Axes of the slice: x: 4 (x_hi: 2, x_lo: 2; x = x_hi * 2 + x_lo), y: 4, z: 16, core: 2. Of those that a mesh axis runs over, the one named last changes fastest.
Arguments:
- ocean_state: bfloat16 [300, 256, 2048], P('ch', 'lat', 'lon'), may hold values from -6 to 6
- land_mask: int32 [256, 2048], P('lat', 'lon'), may hold values 0 or 1
- out_grad: bfloat16 [300, 256, 2048], P('ch', 'lat', 'lon'), may hold values from -6 to 6
- swath_offset: int32 [8, 16, 512], P('lat', 'lon'), may hold values from 0 to 4095
- swath_value: float32 [8, 16, 512], P('lat', 'lon'), may hold values from -8 to 8
- depth_kernel: float32 [3, 3, 300], P(None, None, 'ch'), may hold values from -2.5 to 2.5
- expand_weight: bfloat16 [300, 600], P(None, 'ch'), may hold values from -0.375 to 0.375
- expand_bias: float32 [600], P('ch'), may hold values from -3 to 3
- project_weight: bfloat16 [600, 300], P('ch'), may hold values from -0.25 to 0.25
Outputs:
- state_grad: bfloat16 [300, 256, 2048], P('ch', 'lat', 'lon')
- expand_grad: float32 [300, 600], P(None, 'ch')
- project_grad: float32 [600, 300], P('ch')
- bias_grad: float32 [600], P('ch')
- kernel_grad: float32 [3, 3, 300], P(None, None, 'ch')
Inputs may be any that keep to these rules, and one draw needn't show every extreme that they name: `swath_offset`: position of a swath point in row-major order over the 32 x 128 cells of its device's block.
All inputs are finite; a program needn't handle non-finite values. No bound on the sum of `land_mask` on one device may be relied on, other than what follows from the above.
Results may differ from a plain program's by a relative error of at most 0.014.
Values may be sent and summed in bfloat16 or wider, within the bound.
A program may use at most 64 MiB of HBM per device.

v0:
```python
import math
import jax
import jax.numpy as jnp
from jax import lax
from jax.sharding import PartitionSpec as P

DILATION_STEP = 2


def with_halo(block, sides, width):
    for axis, dim in sides:
        count = lax.axis_size(axis)
        forward = [(i, i + 1) for i in range(count - 1)]
        forward.append((count - 1, 0))
        backward = [(target, source) for source, target in forward]
        low = lax.ppermute(
            lax.slice_in_dim(block, block.shape[dim] - width, None, axis=dim), axis, forward
        )
        high = lax.ppermute(lax.slice_in_dim(block, 0, width, axis=dim), axis, backward)
        block = jnp.concatenate([low, block, high], axis=dim)
    return block


def extend(ocean_field):
    count_of_rows = ocean_field.shape[1]
    column_count = ocean_field.shape[2]
    halo_padded = with_halo(ocean_field, (("lon", 2), ("lat", 1)), DILATION_STEP)
    uppermost_rows = ocean_field[:, count_of_rows - DILATION_STEP :, :]
    gathered = lax.all_gather(uppermost_rows, "lon", axis=2, tiled=True)
    seam_mirrored = gathered[:, ::-1, ::-1]
    seam_mirrored = jnp.concatenate(
        [seam_mirrored[:, :, -DILATION_STEP:], seam_mirrored, seam_mirrored[:, :, :DILATION_STEP]],
        axis=2,
    )
    northern_border = lax.dynamic_slice_in_dim(
        seam_mirrored, lax.axis_index("lon") * column_count, column_count + 2 * DILATION_STEP, 2
    )
    latitude_index = lax.axis_index("lat")
    southern_boundary = halo_padded[:, :DILATION_STEP, :]
    southern_border = jnp.where(
        latitude_index == 0, jnp.zeros_like(southern_boundary), southern_boundary
    )
    northern_border = jnp.where(
        latitude_index == lax.axis_size("lat") - 1,
        northern_border,
        halo_padded[:, count_of_rows + DILATION_STEP :, :],
    )
    return jnp.concatenate(
        [
            southern_border,
            halo_padded[:, DILATION_STEP : count_of_rows + DILATION_STEP, :],
            northern_border,
        ],
        axis=1,
    )


def on_device(
    ocean_state,
    land_mask,
    out_grad,
    swath_offset,
    swath_value,
    depth_kernel,
    expand_weight,
    expand_bias,
    project_weight,
):
    channels_per_shard = ocean_state.shape[0]
    count_of_rows = ocean_state.shape[1]
    column_count = ocean_state.shape[2]
    cells = count_of_rows * column_count
    scale = 1.0 / math.sqrt(
        count_of_rows * lax.axis_size("lat") * column_count * lax.axis_size("lon")
    )
    mask_float = land_mask.astype(jnp.float32)[None]
    masked = ocean_state * land_mask.astype(jnp.bfloat16)[None]
    state_pad = extend(masked)
    forward = jnp.zeros((channels_per_shard, count_of_rows, column_count), jnp.float32)
    for row_offset in range(3):
        for column_offset in range(3):
            kernel_window = state_pad[
                :,
                DILATION_STEP * row_offset : DILATION_STEP * row_offset + count_of_rows,
                DILATION_STEP * column_offset : DILATION_STEP * column_offset + column_count,
            ]
            forward = forward + depth_kernel[row_offset, column_offset][
                :, None, None
            ] * kernel_window.astype(jnp.float32)
    conv_out = forward.astype(jnp.bfloat16)
    swath = (
        jnp.zeros((cells,), jnp.float32).at[swath_offset.reshape(-1)].add(swath_value.reshape(-1))
    )
    first_group = jnp.where(lax.axis_index("ch") == 0, 1.0, 0.0).astype(jnp.float32)
    cotan = (
        out_grad.astype(jnp.float32)
        .at[0]
        .add(first_group * swath.reshape(count_of_rows, column_count))
    )
    cotan = (cotan * mask_float).astype(jnp.bfloat16)
    conv_all, cotan_all = (
        lax.all_gather(conv_out, "ch", axis=0, tiled=True),
        lax.all_gather(cotan, "ch", axis=0, tiled=True),
    )
    conv_flat = conv_all.reshape(conv_all.shape[0], cells)
    cotan_flat = cotan_all.reshape(cotan_all.shape[0], cells)
    hidden = (
        jnp.dot(expand_weight.T, conv_flat, preferred_element_type=jnp.float32)
        + expand_bias[:, None]
    )
    activ, gelu_back = jax.vjp(jax.nn.gelu, hidden)
    act_grad = jnp.dot(project_weight, cotan_flat, preferred_element_type=jnp.float32)
    pre_grad = gelu_back(act_grad)[0].astype(jnp.bfloat16)
    project_part = (
        jnp.dot(activ.astype(jnp.bfloat16), cotan_flat.T, preferred_element_type=jnp.float32)
        * scale
    )
    expand_part = jnp.dot(conv_flat, pre_grad.T, preferred_element_type=jnp.float32) * scale
    bias_part = jnp.sum(pre_grad.astype(jnp.float32), axis=1) * scale
    summed = lax.psum_scatter(
        jnp.dot(expand_weight, pre_grad, preferred_element_type=jnp.float32).astype(jnp.bfloat16),
        "ch",
        scatter_dimension=0,
        tiled=True,
    )
    conv_grad = summed.reshape(channels_per_shard, count_of_rows, column_count)
    grad_pad = extend(conv_grad)
    grad_float = conv_grad.astype(jnp.float32)
    kernel_rows = []
    swapped_axes = jnp.zeros((channels_per_shard, count_of_rows, column_count), jnp.float32)
    for row_offset in range(3):
        kernel_cols = []
        for column_offset in range(3):
            kernel_window = state_pad[
                :,
                DILATION_STEP * row_offset : DILATION_STEP * row_offset + count_of_rows,
                DILATION_STEP * column_offset : DILATION_STEP * column_offset + column_count,
            ]
            kernel_cols.append(jnp.sum(grad_float * kernel_window.astype(jnp.float32), axis=(1, 2)))
            reverse_row = DILATION_STEP * (2 - row_offset)
            reverse_column = DILATION_STEP * (2 - column_offset)
            back_window = grad_pad[
                :,
                reverse_row : reverse_row + count_of_rows,
                reverse_column : reverse_column + column_count,
            ]
            swapped_axes = swapped_axes + depth_kernel[row_offset, column_offset][
                :, None, None
            ] * back_window.astype(jnp.float32)
        kernel_rows.append(jnp.stack(kernel_cols, axis=0))
    kernel_part = jnp.stack(kernel_rows, axis=0) * scale
    fold_adjustment = jnp.zeros((channels_per_shard, DILATION_STEP, column_count), jnp.float32)
    for column_offset in range(3):
        reverse_column = DILATION_STEP * (2 - column_offset)
        rim_window = grad_pad[
            :,
            count_of_rows + DILATION_STEP : count_of_rows + 2 * DILATION_STEP,
            reverse_column : reverse_column + column_count,
        ]
        weight_change = depth_kernel[2, 2 - column_offset] - depth_kernel[0, column_offset]
        fold_adjustment = fold_adjustment + weight_change[:, None, None] * rim_window.astype(
            jnp.float32
        )
    at_top = lax.axis_index("lat") == lax.axis_size("lat") - 1
    swapped_axes = swapped_axes.at[:, count_of_rows - DILATION_STEP :, :].add(
        jnp.where(at_top, fold_adjustment, jnp.zeros_like(fold_adjustment))
    )
    state_grad = (mask_float * (cotan.astype(jnp.float32) + swapped_axes)).astype(jnp.bfloat16)
    expand_grad, project_grad, bias_grad, kernel_grad = lax.psum(
        (expand_part, project_part, bias_part, kernel_part), ("lon", "lat")
    )
    return (state_grad, expand_grad, project_grad, bias_grad, kernel_grad)


def solution(mesh):
    return jax.shard_map(
        on_device,
        mesh=mesh,
        in_specs=(
            P("ch", "lat", "lon"),
            P("lat", "lon"),
            P("ch", "lat", "lon"),
            P("lat", "lon", None),
            P("lat", "lon", None),
            P(None, None, "ch"),
            P(None, "ch"),
            P("ch"),
            P("ch", None),
        ),
        out_specs=(
            P("ch", "lat", "lon"),
            P(None, "ch"),
            P("ch", None),
            P("ch"),
            P(None, None, "ch"),
        ),
        check_vma=False,
    )
```

profile of v0, /device:TPU:4, one launch (start us, length us, event | category | flops | bytes accessed | tf_op | source)
XLA Modules:
  0.0 1292.7 jit_solution(13573045520863102719)
XLA Ops:
  8.7 1.2 convert_element_type.110
  10.0 3.4 scatter_custom_fusion
  16.0 11.4 collective-permute-start.1
  28.2 1.9 collective-permute-start
  30.1 32.5 %all_gather.13 = bf16[75,2,2048]{2,1,0:T(2,128)(2,1)S(1)} all-gather(bf16[75,2,128]{2,1,0:T(2,128)(2,1)S(1)} %slice.277), channel_id=1, replica_groups=mesh['lon'=16,'lat'=8,'ch'=4] {'lon'}, dimensions={2}, use_global_device_ids=true | all-gather | bytes 652800 | tf_op jit(solution)/shard_map/all_gather | solution.py:29
  65.4 3.5 collective-permute-start.2
  69.5 5.5 rev.6
  75.7 4.0 concatenate.54
  79.7 4.5 collective-permute-start.3
  84.2 1.9 collective-permute-done.3
  86.1 1.1 broadcast_select_fusion.1
  87.2 2.4 maximum_maximum_fusion
  89.7 1.1 copy-done.1
  91.3 4.1 fusion.19
  95.6 1.3 dynamic-slice.20
  98.1 2.1 pad.67
  100.3 1.2 copy.42
  101.5 23.7 %all-gather.5.cloned.1.call-done = bf16[300,32,128]{2,1,0:T(8,128)(2,1)} async-done(((bf16[75,32,128]{2,1,0:T(8,128)(2,1)}), bf16[300,32,128]{2,1,0:T(8,128)(2,1)}) %all-gather.5.cloned.1.call-update) | async-done | bytes 2457616 | tf_op jit(solution)/shard_map/all_gather | solution.py:102
  125.2 2.1 pad.68
  127.3 1.2 copy.43
  129.4 1.9 fusion.34
  131.3 2.5 convert_reduce_fusion
  133.9 1.1 copy-done.11
  134.9 1.8 convolution_multiply_fusion
  136.7 2.2 fusion.2
  138.9 31.6 %fusion = bf16[80,4096]{1,0:T(8,128)(2,1)} fusion(bf16[300,4096]{1,0:T(8,128)(2,1)S(1)} %fusion.2), kind=kCustom, calls=%all-reduce-scatter | all-reduce-scatter fusion | flops 1310721 | bytes 3115008
  171.4 1.9 collective-permute-start.8
  173.9 5.3 collective-permute-done.8
  179.2 6.0 concatenate.62
  185.2 1.4 constant_dynamic-slice_fusion
  186.9 4.9 fusion.28
  192.2 34.5 %all_gather.15 = bf16[75,2,2048]{2,1,0:T(2,128)(2,1)S(1)} all-gather(bf16[75,2,128]{2,1,0:T(2,128)(2,1)S(1)} %slice.285), channel_id=1, replica_groups=mesh['lon'=16,'lat'=8,'ch'=4] {'lon'}, dimensions={2}, use_global_device_ids=true | all-gather | bytes 652800 | tf_op jit(solution)/shard_map/all_gather | solution.py:29
  228.3 3.0 collective-permute-start.5
  231.3 2.8 collective-permute-start.4
  234.4 3.8 collective-permute-done.4
  240.7 3.2 collective-permute-start.7
  244.0 5.5 rev.7
  250.1 4.0 concatenate.57
  254.2 311.0 %all-reduce.2 = (f32[150]{0:T(256)}, f32[3,3,75]{2,1,0:T(4,128)}) all-reduce(f32[150]{0:T(256)S(1)} %copy-done.33, f32[3,3,75]{2,1,0:T(4,128)S(1)} %maximum_multiply_fusion), channel_id=1, replica_groups=mesh['lon'=16,'lat'=8,'ch'=4] {'lon','lat'}, use_global_device_ids=true, to_apply=%region_5.6 | all-reduce | flops 825 | bytes 6600 | tf_op jit(solution)/shard_map/psum | solution.py:169
  565.2 1.9 collective-permute-start.6
  567.2 4.3 collective-permute-done.6
  571.5 1.1 broadcast_select_fusion
  572.6 2.4 pad_maximum_fusion.1
  575.2 3.4 fusion.24
  579.0 1.1 multiply_convert_fusion.2
  580.2 702.8 %all-reduce.6.cloned.1.call-done = (f32[300,150]{0,1:T(8,128)}, f32[150,300]{1,0:T(8,128)}) async-done(((f32[300,150]{0,1:T(8,128)}, f32[150,300]{1,0:T(8,128)}), (f32[300,150]{0,1:T(8,128)}, f32[150,300]{1,0:T(8,128)})) %all-reduce.6.cloned.1.call-update) | async-done | bytes 360016 | tf_op jit(solution)/shard_map/psum | solution.py:169
  1282.9 1.6 copy.49
  1284.6 1.6 copy.50
  (142 shorter events, 18.8 us)
Async XLA Ops:
  7.2 121.4 %copy-start = (bf16[300,150]{0,1:T(8,128)(2,1)S(1)}, bf16[300,150]{0,1:T(8,128)(2,1)}, u32[]{:S(2)}) copy-start(bf16[300,150]{0,1:T(8,128)(2,1)} %param.19) | copy-start | bytes 270004
  7.2 91.0 %all-gather.3.cloned.1.call-start = ((), (), s32[]{:S(2)}) async-start(), calls=%async_computation | async-start | bytes 3072000 | tf_op jit(solution)/shard_map/all_gather | solution.py:103
  14.4 110.8 %all-gather.5.cloned.1.call-start = ((), (), s32[]{:S(2)}) async-start(), calls=%async_computation.1 | async-start | bytes 3072000 | tf_op jit(solution)/shard_map/all_gather | solution.py:102
  16.0 47.9 %collective-permute-start.1 = (bf16[75,32,2]{0,1,2:T(8,128)(2,1)S(1)}, bf16[75,32,2]{0,1,2:T(8,128)(2,1)S(1)}, u32[]{:S(2)}, u32[]{:S(2)}) collective-permute-start(bf16[75,32,2]{0,1,2:T(8,128)(2,1)S(1)} %copy.31), channel_id=1, source_target_pairs={{32,0},{64,32},{96,64},{128,96},{160,128},{192,160},{224,192},{256... | collective-permute-start | bytes 28808 | tf_op jit(solution)/shard_map/ppermute | solution.py:19
  28.2 34.6 %collective-permute-start = (bf16[75,32,2]{0,1,2:T(8,128)(2,1)S(1)}, bf16[75,32,2]{0,1,2:T(8,128)(2,1)S(1)}, u32[]{:S(2)}, u32[]{:S(2)}) collective-permute-start(bf16[75,32,2]{0,1,2:T(8,128)(2,1)S(1)} %copy.30), channel_id=1, source_target_pairs={{0,32},{32,64},{64,96},{96,128},{128,160},{160,192},{192,224},{224... | collective-permute-start | bytes 28808 | tf_op jit(solution)/shard_map/ppermute | solution.py:16
  63.8 25.8 %copy-start.5 = (bf16[75,32,2]{2,1,0:T(8,128)(2,1)}, bf16[75,32,2]{2,1,0:T(8,128)(2,1)S(1)}, u32[]{:S(2)}) copy-start(bf16[75,32,2]{2,1,0:T(8,128)(2,1)S(1)} %copy.32) | copy-start | bytes 28804
  63.8 5.0 copy-start.13
  64.9 24.7 %copy-start.7 = (bf16[75,32,2]{2,1,0:T(8,128)(2,1)}, bf16[75,32,2]{2,1,0:T(8,128)(2,1)S(1)}, u32[]{:S(2)}) copy-start(bf16[75,32,2]{2,1,0:T(8,128)(2,1)S(1)} %copy.33) | copy-start | bytes 28804
  65.4 18.8 %collective-permute-start.2 = (bf16[75,2,132]{2,1,0:T(2,128)(2,1)S(1)}, bf16[75,2,132]{2,1,0:T(2,128)(2,1)}, u32[]{:S(2)}, u32[]{:S(2)}) collective-permute-start(bf16[75,2,132]{2,1,0:T(2,128)(2,1)S(1)} %get-tuple-element.51), channel_id=1, source_target_pairs={{0,4},{4,8},{8,12},{12,16},{16,20},{20,24},{24,28},{28,0},{1,5},{5... | collective-permute-start | bytes 118808 | tf_op jit(solution)/shard_map/ppermute | solution.py:16
  69.5 20.2 %copy-start.14 = (f32[75]{0:T(128)}, f32[75]{0:T(128)S(1)}, u32[]{:S(2)}) copy-start(f32[75]{0:T(128)S(1)} %get-tuple-element.72) | copy-start | bytes 904
  69.5 20.2 %copy-start.16 = (f32[75]{0:T(128)}, f32[75]{0:T(128)S(1)}, u32[]{:S(2)}) copy-start(f32[75]{0:T(128)S(1)} %get-tuple-element.73) | copy-start | bytes 904
  69.5 20.2 %copy-start.18 = (f32[75]{0:T(128)}, f32[75]{0:T(128)S(1)}, u32[]{:S(2)}) copy-start(f32[75]{0:T(128)S(1)} %get-tuple-element.74) | copy-start | bytes 904
  69.5 20.2 %copy-start.20 = (f32[75]{0:T(128)}, f32[75]{0:T(128)S(1)}, u32[]{:S(2)}) copy-start(f32[75]{0:T(128)S(1)} %get-tuple-element.75) | copy-start | bytes 904
  69.5 20.2 %copy-start.22 = (f32[75]{0:T(128)}, f32[75]{0:T(128)S(1)}, u32[]{:S(2)}) copy-start(f32[75]{0:T(128)S(1)} %get-tuple-element.76) | copy-start | bytes 904
  69.5 20.2 %copy-start.24 = (f32[75]{0:T(128)}, f32[75]{0:T(128)S(1)}, u32[]{:S(2)}) copy-start(f32[75]{0:T(128)S(1)} %get-tuple-element.77) | copy-start | bytes 904
  79.7 6.5 collective-permute-start.3
  87.2 4.1 copy-start.26
  87.2 4.1 copy-start.28
  87.2 4.1 copy-start.30
  95.4 1187.5 %all-reduce.6.cloned.1.call-start = ((), (), s32[]{:S(2)}) async-start(), calls=%async_computation.2 | async-start | bytes 933888 | tf_op jit(solution)/shard_map/psum | solution.py:169
  171.4 7.8 collective-permute-start.8
  173.3 13.4 %copy-start.8 = (bf16[75,32,2]{2,1,0:T(8,128)(2,1)S(1)}, bf16[75,32,2]{2,1,0:T(8,128)(2,1)}, u32[]{:S(2)}) copy-start(bf16[75,32,2]{2,1,0:T(8,128)(2,1)} %copy-done.7) | copy-start | bytes 28804
  179.2 7.5 copy-start.4
  192.1 42.1 %copy-start.34 = (f32[75]{0:T(128)S(1)}, f32[75]{0:T(128)}, u32[]{:S(2)}) copy-start(f32[75]{0:T(128)} %get-tuple-element.35) | copy-start | bytes 904
  192.1 42.1 %copy-start.35 = (f32[75]{0:T(128)S(1)}, f32[75]{0:T(128)}, u32[]{:S(2)}) copy-start(f32[75]{0:T(128)} %get-tuple-element.36) | copy-start | bytes 904
  192.1 42.1 %copy-start.36 = (f32[75]{0:T(128)S(1)}, f32[75]{0:T(128)}, u32[]{:S(2)}) copy-start(f32[75]{0:T(128)} %get-tuple-element.37) | copy-start | bytes 904
  192.1 42.1 %copy-start.37 = (f32[75]{0:T(128)S(1)}, f32[75]{0:T(128)}, u32[]{:S(2)}) copy-start(f32[75]{0:T(128)} %get-tuple-element.56) | copy-start | bytes 904
  192.1 42.1 %copy-start.38 = (f32[75]{0:T(128)S(1)}, f32[75]{0:T(128)}, u32[]{:S(2)}) copy-start(f32[75]{0:T(128)} %get-tuple-element.57) | copy-start | bytes 904
  192.1 42.1 %copy-start.39 = (f32[75]{0:T(128)S(1)}, f32[75]{0:T(128)}, u32[]{:S(2)}) copy-start(f32[75]{0:T(128)} %get-tuple-element.58) | copy-start | bytes 904
  192.1 42.1 %copy-start.43 = (f32[75]{0:T(128)S(1)}, f32[75]{0:T(128)}, u32[]{:S(2)}) copy-start(f32[75]{0:T(128)} %get-tuple-element.53) | copy-start | bytes 904
  192.2 42.1 %copy-start.44 = (f32[75]{0:T(128)S(1)}, f32[75]{0:T(128)}, u32[]{:S(2)}) copy-start(f32[75]{0:T(128)} %get-tuple-element.54) | copy-start | bytes 904
  192.2 42.1 %copy-start.45 = (f32[75]{0:T(128)S(1)}, f32[75]{0:T(128)}, u32[]{:S(2)}) copy-start(f32[75]{0:T(128)} %get-tuple-element.55) | copy-start | bytes 904
  228.3 10.9 collective-permute-start.5
  231.3 6.8 collective-permute-start.4
  240.7 326.4 %collective-permute-start.7 = (bf16[75,2,132]{2,1,0:T(2,128)(2,1)S(1)}, bf16[75,2,132]{2,1,0:T(2,128)(2,1)}, u32[]{:S(2)}, u32[]{:S(2)}) collective-permute-start(bf16[75,2,132]{2,1,0:T(2,128)(2,1)S(1)} %get-tuple-element.48), channel_id=1, source_target_pairs={{0,4},{4,8},{8,12},{12,16},{16,20},{20,24},{24,28},{28,0},{1,5},{5... | collective-permute-start | bytes 118808 | tf_op jit(solution)/shard_map/ppermute | solution.py:16
  244.0 10.2 copy-start.33
  565.2 6.3 collective-permute-start.6
  572.5 2.5 copy-start.15
  572.5 2.5 copy-start.17
  572.5 2.5 copy-start.19
  572.6 2.5 copy-start.21
  572.6 2.5 copy-start.23
  572.6 2.5 copy-start.25
  572.6 2.5 copy-start.27
  575.1 3.4 copy-start.40
  575.2 3.4 copy-start.41
  575.2 3.4 copy-start.42
  575.2 3.9 copy-start.10
  (11 other events, 18.3 us)
Sparse Core Ops, SparseCore 0:
  14.5 38.0 all-gather.2
  95.5 29.6 all-gather.4
  173.5 1109.3 all-reduce.5
where the time goes:
time: 1290 us
  waiting for transfers between devices  742 us (58%)
  blocking collectives  410 us (32%)
  local copies, waits for them, and re-layouts  52.1 us (4%)
  starting transfers between devices  34.4 us (3%)
  other arithmetic  30.2 us (2%)
  between operations  15.4 us (1%)
    psum x1, waiting for transfers between devices, on_device(): lax.psum((expand_part, project_part, bias_part, kernel_part), ('lon', 'la...  703 us
    psum x1, blocking collectives, on_device(): lax.psum((expand_part, project_part, bias_part, kernel_part), ('lon', 'la...  311 us
    all_gather x2, blocking collectives, extend(): gathered = lax.all_gather(uppermost_rows, 'lon', axis=2, tiled=True)  67 us
    unnamed x1, blocking collectives  31.6 us
  transfers between devices with their start and end apart: 12, of which 6 were waited for; matrix products, arithmetic and copies ran while one was open for 5% of the time, Pallas kernels for 0%

commit v1 on v0

--- a/solution.py
+++ b/solution.py
@@ -26,7 +26,9 @@
     column_count = ocean_field.shape[2]
     halo_padded = with_halo(ocean_field, (("lon", 2), ("lat", 1)), DILATION_STEP)
     uppermost_rows = ocean_field[:, count_of_rows - DILATION_STEP :, :]
-    gathered = lax.all_gather(uppermost_rows, "lon", axis=2, tiled=True)
+    gathered = jnp.concatenate(
+        lax.all_to_all(jnp.stack([uppermost_rows] * lax.axis_size("lon")), "lon", 0, 0), axis=2
+    )
     seam_mirrored = gathered[:, ::-1, ::-1]
     seam_mirrored = jnp.concatenate(
         [seam_mirrored[:, :, -DILATION_STEP:], seam_mirrored, seam_mirrored[:, :, :DILATION_STEP]],

time: 1290 us -> 1320 us (1.023)
  blocking collectives: 410 us -> 346 us
  waiting for transfers between devices: 742 us -> 790 us
  starting transfers between devices: 34.4 us -> 57.6 us
    all_gather x2 -> x0, blocking collectives: 67 us -> none  [extend(): gathered = lax.all_gather(uppermost_rows, 'lon', axis=2, tiled=True)]
    psum x1, waiting for transfers between devices: 703 us -> 745 us  [on_device(): lax.psum((expand_part, project_part, bias_part, kernel_part), ('lon', 'la...]
    all_to_all x0 -> x2, starting transfers between devices: none -> 27.5 us  [extend(): lax.all_to_all(jnp.stack([uppermost_rows] * lax.axis_size('lon')), 'lon',...]
  transfers between devices with their start and end apart: 12 -> 14, of which waited for: 6 -> 5; matrix products, arithmetic and copies ran while one was open for 5% -> 6% of each run, Pallas kernels for 0% -> 0%
where the time goes in v1:
time: 1320 us
  waiting for transfers between devices  790 us (60%)
  blocking collectives  346 us (26%)
  local copies, waits for them, and re-layouts  64.8 us (5%)
  starting transfers between devices  57.6 us (4%)
  other arithmetic  32 us (2%)
  between operations  15.4 us (1%)
    psum x1, waiting for transfers between devices, on_device(): lax.psum((expand_part, project_part, bias_part, kernel_part), ('lon', 'la...  745 us
    psum x1, blocking collectives, on_device(): lax.psum((expand_part, project_part, bias_part, kernel_part), ('lon', 'la...  314 us
    unnamed x1, blocking collectives  32 us
    all_to_all x2, starting transfers between devices, extend(): lax.all_to_all(jnp.stack([uppermost_rows] * lax.axis_size('lon')), 'lon',...  27.5 us
  transfers between devices with their start and end apart: 14, of which 5 were waited for; matrix products, arithmetic and copies ran while one was open for 6% of the time, Pallas kernels for 0%

profile of v1, /device:TPU:4, one launch (start us, length us, event | category | flops | bytes accessed | tf_op | source)
XLA Modules:
  0.0 1317.7 jit_solution(15743403185017212462)
XLA Ops:
  10.3 15.2 %all-to-all-start = ((bf16[16,75,2,128]{3,2,1,0:T(2,128)(2,1)}), bf16[16,75,2,128]{3,2,1,0:T(2,128)(2,1)S(1)}, u32[]{:S(2)}, u32[]{:S(2)}) async-start(bf16[16,75,2,128]{3,2,1,0:T(2,128)(2,1)} %stack.36), calls=%async_computation | async-start | bytes 1228800 | tf_op jit(solution)/shard_map/all_to_all | solution.py:30
  25.8 3.4 scatter_custom_fusion
  31.5 1.8 copy.14
  33.2 3.8 collective-permute-start
  37.8 3.2 collective-permute-start.1
  41.0 12.9 collective-permute-done
  56.6 3.5 collective-permute-start.2
  60.6 4.6 collective-permute-start.3
  65.3 1.3 collective-permute-done.2
  67.2 5.5 rev.6
  73.3 4.0 concatenate.54
  78.4 2.4 maximum_maximum_fusion
  82.6 4.1 fusion.19
  86.7 1.3 dynamic-slice.20
  88.7 2.1 pad.67
  90.8 2.6 copy.30
  93.5 25.3 %all-gather.5.cloned.1.call-done = bf16[300,32,128]{2,1,0:T(8,128)(2,1)} async-done(((bf16[75,32,128]{2,1,0:T(8,128)(2,1)}), bf16[300,32,128]{2,1,0:T(8,128)(2,1)}) %all-gather.5.cloned.1.call-update) | async-done | bytes 2457616 | tf_op jit(solution)/shard_map/all_gather | solution.py:104
  118.8 2.1 pad.68
  120.9 1.2 copy.31
  123.9 2.5 convert_reduce_fusion
  127.4 2.3 fusion.2
  129.7 32.0 %fusion = bf16[80,4096]{1,0:T(8,128)(2,1)} fusion(bf16[300,4096]{1,0:T(8,128)(2,1)} %fusion.2), kind=kCustom, calls=%all-reduce-scatter | all-reduce-scatter fusion | flops 1310721 | bytes 3115008
  162.7 2.1 collective-permute-start.8
  165.4 5.0 collective-permute-done.8
  170.4 6.0 concatenate.62
  176.4 1.3 constant_dynamic-slice_fusion
  179.9 12.3 all-to-all-start.1
  192.3 3.2 convolution_multiply_fusion
  195.5 3.7 fusion.34
  199.8 1.2 fusion.46
  201.1 1.9 copy.21
  202.9 1.8 copy.22
  204.7 5.1 collective-permute-start.5
  209.8 1.9 collective-permute-start.4
  211.8 7.2 fusion.28
  219.1 1.8 copy.23
  220.8 1.8 copy.24
  223.1 3.4 collective-permute-start.7
  226.5 313.8 %all-reduce.2 = (f32[150]{0:T(256)}, f32[3,3,75]{2,1,0:T(4,128)}) all-reduce(f32[150]{0:T(256)S(1)} %copy-done.38, f32[3,3,75]{2,1,0:T(4,128)S(1)} %maximum_multiply_fusion), channel_id=1, replica_groups=mesh['lon'=16,'lat'=8,'ch'=4] {'lon','lat'}, use_global_device_ids=true, to_apply=%region_5.6 | all-reduce | flops 825 | bytes 6600 | tf_op jit(solution)/shard_map/psum | solution.py:171
  540.3 2.2 collective-permute-start.6
  542.5 1.5 copy_bitcast_fusion
  544.2 5.5 rev.7
  550.3 4.0 concatenate.57
  555.5 2.4 pad_maximum_fusion.1
  558.1 3.4 fusion.24
  563.0 744.8 %all-reduce.6.cloned.1.call-done = (f32[300,150]{0,1:T(8,128)}, f32[150,300]{1,0:T(8,128)}) async-done(((f32[300,150]{0,1:T(8,128)}, f32[150,300]{1,0:T(8,128)}), (f32[300,150]{0,1:T(8,128)}, f32[150,300]{1,0:T(8,128)})) %all-reduce.6.cloned.1.call-update) | async-done | bytes 360016 | tf_op jit(solution)/shard_map/psum | solution.py:171
  1307.9 1.6 copy.39
  1309.5 1.6 copy.40
  (142 shorter events, 24.6 us)
Async XLA Ops:
  7.2 115.0 %copy-start = (bf16[300,150]{0,1:T(8,128)(2,1)S(1)}, bf16[300,150]{0,1:T(8,128)(2,1)}, u32[]{:S(2)}) copy-start(bf16[300,150]{0,1:T(8,128)(2,1)} %param.19) | copy-start | bytes 270004
  9.1 16.5 %copy-start.42 = (s32[1,1,512]{2,1,0:T(1,128)S(1)}, s32[1,1,512]{2,1,0:T(1,128)}, u32[]{:S(2)}) copy-start(s32[1,1,512]{2,1,0:T(1,128)} %param.16) | copy-start | bytes 6148
  9.1 16.5 %copy-start.17 = (bf16[75,32,128]{2,1,0:T(8,128)(2,1)S(1)}, bf16[75,32,128]{2,1,0:T(8,128)(2,1)}, u32[]{:S(2)}) copy-start(bf16[75,32,128]{2,1,0:T(8,128)(2,1)} %param.15) | copy-start | bytes 1843204
  10.3 56.3 %all-to-all-start = ((bf16[16,75,2,128]{3,2,1,0:T(2,128)(2,1)}), bf16[16,75,2,128]{3,2,1,0:T(2,128)(2,1)S(1)}, u32[]{:S(2)}, u32[]{:S(2)}) async-start(bf16[16,75,2,128]{3,2,1,0:T(2,128)(2,1)} %stack.36), calls=%async_computation | async-start | bytes 1228800 | tf_op jit(solution)/shard_map/all_to_all | solution.py:30
  25.5 63.2 %all-gather.3.cloned.1.call-start = ((), (), s32[]{:S(2)}) async-start(), calls=%async_computation.2 | async-start | bytes 3072000 | tf_op jit(solution)/shard_map/all_gather | solution.py:105
  30.3 88.5 %all-gather.5.cloned.1.call-start = ((), (), s32[]{:S(2)}) async-start(), calls=%async_computation.3 | async-start | bytes 3072000 | tf_op jit(solution)/shard_map/all_gather | solution.py:104
  33.2 20.7 %collective-permute-start = (bf16[75,32,2]{0,1,2:T(8,128)(2,1)S(1)}, bf16[75,32,2]{0,1,2:T(8,128)(2,1)S(1)}, u32[]{:S(2)}, u32[]{:S(2)}) collective-permute-start(bf16[75,32,2]{0,1,2:T(8,128)(2,1)S(1)} %copy.14), channel_id=1, source_target_pairs={{0,32},{32,64},{64,96},{96,128},{128,160},{160,192},{192,224},{224... | collective-permute-start | bytes 28808 | tf_op jit(solution)/shard_map/ppermute | solution.py:16
  37.8 17.2 %collective-permute-start.1 = (bf16[75,32,2]{0,1,2:T(8,128)(2,1)S(1)}, bf16[75,32,2]{0,1,2:T(8,128)(2,1)S(1)}, u32[]{:S(2)}, u32[]{:S(2)}) collective-permute-start(bf16[75,32,2]{0,1,2:T(8,128)(2,1)S(1)} %copy.15), channel_id=1, source_target_pairs={{32,0},{64,32},{96,64},{128,96},{160,128},{192,160},{224,192},{256... | collective-permute-start | bytes 28808 | tf_op jit(solution)/shard_map/ppermute | solution.py:19
  55.0 25.9 %copy-start.4 = (bf16[75,32,2]{2,1,0:T(8,128)(2,1)}, bf16[75,32,2]{2,1,0:T(8,128)(2,1)S(1)}, u32[]{:S(2)}) copy-start(bf16[75,32,2]{2,1,0:T(8,128)(2,1)S(1)} %copy.16) | copy-start | bytes 28804
  55.0 5.0 copy-start.18
  56.1 24.8 %copy-start.6 = (bf16[75,32,2]{2,1,0:T(8,128)(2,1)}, bf16[75,32,2]{2,1,0:T(8,128)(2,1)S(1)}, u32[]{:S(2)}) copy-start(bf16[75,32,2]{2,1,0:T(8,128)(2,1)S(1)} %copy.17) | copy-start | bytes 28804
  56.6 10.0 collective-permute-start.2
  60.6 20.3 %copy-start.19 = (f32[75]{0:T(128)}, f32[75]{0:T(128)S(1)}, u32[]{:S(2)}) copy-start(f32[75]{0:T(128)S(1)} %get-tuple-element.72) | copy-start | bytes 904
  60.6 20.3 %copy-start.21 = (f32[75]{0:T(128)}, f32[75]{0:T(128)S(1)}, u32[]{:S(2)}) copy-start(f32[75]{0:T(128)S(1)} %get-tuple-element.73) | copy-start | bytes 904
  60.6 20.3 %copy-start.23 = (f32[75]{0:T(128)}, f32[75]{0:T(128)S(1)}, u32[]{:S(2)}) copy-start(f32[75]{0:T(128)S(1)} %get-tuple-element.74) | copy-start | bytes 904
  60.6 20.3 %copy-start.25 = (f32[75]{0:T(128)}, f32[75]{0:T(128)S(1)}, u32[]{:S(2)}) copy-start(f32[75]{0:T(128)S(1)} %get-tuple-element.75) | copy-start | bytes 904
  60.6 20.3 %copy-start.27 = (f32[75]{0:T(128)}, f32[75]{0:T(128)S(1)}, u32[]{:S(2)}) copy-start(f32[75]{0:T(128)S(1)} %get-tuple-element.76) | copy-start | bytes 904
  60.6 20.3 %copy-start.29 = (f32[75]{0:T(128)}, f32[75]{0:T(128)S(1)}, u32[]{:S(2)}) copy-start(f32[75]{0:T(128)S(1)} %get-tuple-element.77) | copy-start | bytes 904
  60.6 16.7 %collective-permute-start.3 = (bf16[75,2,132]{2,1,0:T(2,128)(2,1)S(1)}, bf16[75,2,132]{2,1,0:T(2,128)(2,1)}, u32[]{:S(2)}, u32[]{:S(2)}) collective-permute-start(bf16[75,2,132]{2,1,0:T(2,128)(2,1)S(1)} %get-tuple-element.52), channel_id=1, source_target_pairs={{4,0},{8,4},{12,8},{16,12},{20,16},{24,20},{28,24},{0,28},{5,1},{9... | collective-permute-start | bytes 118808 | tf_op jit(solution)/shard_map/ppermute | solution.py:19
  78.4 4.2 copy-start.31
  78.4 4.2 copy-start.33
  78.4 4.2 copy-start.35
  123.0 3.4 copy-start.14
  162.7 7.8 collective-permute-start.8
  179.9 362.7 %all-to-all-start.1 = ((bf16[16,75,2,128]{3,2,1,0:T(2,128)(2,1)}), bf16[16,75,2,128]{3,2,1,0:T(2,128)(2,1)}, u32[]{:S(2)}, u32[]{:S(2)}) async-start(bf16[16,75,2,128]{3,2,1,0:T(2,128)(2,1)} %stack.37), calls=%async_computation.1 | async-start | bytes 1228800 | tf_op jit(solution)/shard_map/all_to_all | solution.py:30
  192.2 1115.7 %all-reduce.6.cloned.1.call-start = ((), (), s32[]{:S(2)}) async-start(), calls=%async_computation.4 | async-start | bytes 933888 | tf_op jit(solution)/shard_map/psum | solution.py:171
  192.3 3.3 copy-start.15
  195.5 4.3 copy-start.9
  199.8 11.9 copy-start.2
  201.1 10.7 copy-start.5
  201.1 10.7 copy-start.7
  204.7 14.3 %copy-start.10 = (bf16[10,8,32,128]{3,2,1,0:T(8,128)(2,1)S(1)}, bf16[10,8,32,128]{3,2,1,0:T(8,128)(2,1)}, u32[]{:S(2)}) copy-start(bf16[10,8,32,128]{3,2,1,0:T(8,128)(2,1)} %copy-done.8) | copy-start | bytes 1966084
  204.7 16.2 %collective-permute-start.5 = (bf16[75,32,2]{0,1,2:T(8,128)(2,1)S(1)}, bf16[75,32,2]{0,1,2:T(8,128)(2,1)}, u32[]{:S(2)}, u32[]{:S(2)}) collective-permute-start(bf16[75,32,2]{0,1,2:T(8,128)(2,1)S(1)} %copy.22), channel_id=1, source_target_pairs={{32,0},{64,32},{96,64},{128,96},{160,128},{192,160},{224,192},{256... | collective-permute-start | bytes 28808 | tf_op jit(solution)/shard_map/ppermute | solution.py:19
  209.8 9.2 collective-permute-start.4
  220.8 5.7 copy-start.38
  223.1 319.4 %collective-permute-start.7 = (bf16[75,2,132]{2,1,0:T(2,128)(2,1)S(1)}, bf16[75,2,132]{2,1,0:T(2,128)(2,1)S(1)}, u32[]{:S(2)}, u32[]{:S(2)}) collective-permute-start(bf16[75,2,132]{2,1,0:T(2,128)(2,1)S(1)} %get-tuple-element.48), channel_id=1, source_target_pairs={{0,4},{4,8},{8,12},{12,16},{16,20},{20,24},{24,28},{28,0},{1,5},{5... | collective-permute-start | bytes 118808 | tf_op jit(solution)/shard_map/ppermute | solution.py:16
  540.3 14.0 %collective-permute-start.6 = (bf16[75,2,132]{2,1,0:T(2,128)(2,1)S(1)}, bf16[75,2,132]{2,1,0:T(2,128)(2,1)}, u32[]{:S(2)}, u32[]{:S(2)}) collective-permute-start(bf16[75,2,132]{2,1,0:T(2,128)(2,1)S(1)} %get-tuple-element.47), channel_id=1, source_target_pairs={{4,0},{8,4},{12,8},{16,12},{20,16},{24,20},{28,24},{0,28},{5,1},{9... | collective-permute-start | bytes 118808 | tf_op jit(solution)/shard_map/ppermute | solution.py:19
  555.4 2.5 copy-start.20
  555.4 2.5 copy-start.22
  555.4 2.5 copy-start.24
  555.5 2.5 copy-start.26
  555.5 2.5 copy-start.28
  555.5 2.5 copy-start.30
  555.5 2.5 copy-start.32
  558.0 3.4 copy-start.39
  558.0 3.4 copy-start.40
  558.1 3.4 copy-start.41
  558.1 3.9 copy-start.12
  (10 other events, 16.7 us)
Sparse Core Ops, SparseCore 0:
  30.5 35.2 all-gather.2
  86.9 31.9 all-gather.4
  199.4 1108.4 all-reduce.5
